TPU v7x, 768 devices: a whole 4x8x12 slice. The times are simulated.
768 devices in a mesh: seq: 96 (over y, z), head: 8 (over x, core).
Axes of the slice: x: 4, y: 8, z: 12, core: 2. Of those that a mesh axis runs over, the one named last changes fastest.
Arguments:
- queries: bfloat16 [12288, 2048], P('seq', 'head'), may hold values from -6 to 6
- keys: bfloat16 [12288, 2048], P('seq', 'head'), may hold values from -6 to 6
- values: bfloat16 [12288, 2048], P('seq', 'head'), may hold values from -6 to 6
- grad_out: bfloat16 [12288, 2048], P('seq', 'head'), may hold values from -6 to 6
- gain: float32 [2048], P('head'), may hold values from 0.1 to 1.9
- segment_ids: int32 [96, 128], P('seq'), may hold values from 0 to 7, never falling along the last dimension, each value on 1 to 32 neighbouring positions
Outputs:
- output: bfloat16 [12288, 2048], P('seq', 'head')
- grad_queries: bfloat16 [12288, 2048], P('seq', 'head')
- grad_keys: bfloat16 [12288, 2048], P('seq', 'head')
- grad_values: bfloat16 [12288, 2048], P('seq', 'head')
Inputs may be any that keep to these rules, and one draw needn't show every extreme that they name: `segment_ids`: ids never fall along a group; each mask block holds 1 to 32 tokens, one exactly 32.
All inputs are finite; a program needn't handle non-finite values.
Results may differ from a plain program's by a relative error of at most 0.0058.
Values sent between devices are 32-bit elements; how exact they have to be, the bound alone decides.
No kernel may reach another device: no remote copies, remote signals or barrier semaphores. Data moves between devices by JAX's collectives and lax.ppermute only.
A program may use at most 32 MiB of HBM per device.

v0:
```python
import jax
import jax.numpy as jnp
from jax import lax
from jax.sharding import PartitionSpec as P

HD = 128
D = 2048


def carried_in(value, axis, combine, identity):
    count, position = (lax.axis_size(axis), lax.axis_index(axis))
    everything = lax.all_gather(value, axis)
    start = jnp.broadcast_to(jnp.asarray(identity, value.dtype), value.shape)

    def turn(k, before):
        reached = k < position
        new = combine(before, everything[k])
        return jnp.where(reached, new, before)

    return lax.fori_loop(0, count, turn, start)


def add_states(earlier, later_term):
    return earlier + later_term


def on_device(queries, keys, values, grad_out, gain, segment_ids):
    length = queries.shape[0]
    width = queries.shape[1]
    heads_here = width // HD
    queries_h = queries.reshape(length, heads_here, HD)
    keys_h = keys.reshape(length, heads_here, HD)
    values_h = values.reshape(length, heads_here, HD)
    segment = segment_ids[0]
    row_ids = lax.broadcasted_iota(jnp.int32, (length, length), 0)
    col_ids = lax.broadcasted_iota(jnp.int32, (length, length), 1)
    allowed = jnp.where(
        (segment[:, None] == segment[None, :]) & (col_ids <= row_ids), 1.0, 0.0
    ).astype(jnp.float32)
    raw_scores = jnp.einsum("thd,shd->hts", queries_h, keys_h, preferred_element_type=jnp.float32)
    scores = (raw_scores * allowed[None]).astype(jnp.bfloat16)
    local_state = jnp.einsum("thd,the->hde", keys_h, values_h, preferred_element_type=jnp.float32)
    zero_state = jnp.zeros_like(local_state)
    state = carried_in(local_state, "seq", add_states, zero_state)
    state_b = state.astype(jnp.bfloat16)
    attn = jnp.einsum("hts,she->the", scores, values_h, preferred_element_type=jnp.float32)
    attn = attn + jnp.einsum("thd,hde->the", queries_h, state_b, preferred_element_type=jnp.float32)
    flat = attn.reshape(length, width)
    gained = gain * grad_out.astype(jnp.float32)
    squares, products = lax.psum(
        (jnp.sum(flat * flat, axis=1), jnp.sum(gained * flat, axis=1)), "head"
    )
    inverse = lax.rsqrt(squares / D + 1e-06)
    output = (gain * flat * inverse[:, None]).astype(jnp.bfloat16)
    dflat = gained * inverse[:, None] - flat * (products * inverse**3 / D)[:, None]
    dattn = dflat.astype(jnp.bfloat16).reshape(length, heads_here, HD)
    grad_local = jnp.einsum("thd,the->hde", queries_h, dattn, preferred_element_type=jnp.float32)
    overall = lax.psum(grad_local, "seq")
    before = carried_in(grad_local, "seq", add_states, zero_state)
    later = overall - before - grad_local
    later_b = later.astype(jnp.bfloat16)
    dscores = (
        jnp.einsum("the,she->hts", dattn, values_h, preferred_element_type=jnp.float32)
        * allowed[None]
    ).astype(jnp.bfloat16)
    grad_q = jnp.einsum("hts,shd->thd", dscores, keys_h, preferred_element_type=jnp.float32)
    grad_q = grad_q + jnp.einsum("the,hde->thd", dattn, state_b, preferred_element_type=jnp.float32)
    grad_k = jnp.einsum("hts,thd->shd", dscores, queries_h, preferred_element_type=jnp.float32)
    grad_k = grad_k + jnp.einsum(
        "she,hde->shd", values_h, later_b, preferred_element_type=jnp.float32
    )
    grad_v = jnp.einsum("hts,the->she", scores, dattn, preferred_element_type=jnp.float32)
    grad_v = grad_v + jnp.einsum(
        "shd,hde->she", keys_h, later_b, preferred_element_type=jnp.float32
    )
    return (
        output,
        grad_q.reshape(length, width).astype(jnp.bfloat16),
        grad_k.reshape(length, width).astype(jnp.bfloat16),
        grad_v.reshape(length, width).astype(jnp.bfloat16),
    )


def solution(mesh):
    placed = (
        P("seq", "head"),
        P("seq", "head"),
        P("seq", "head"),
        P("seq", "head"),
        P("head"),
        P("seq", None),
    )
    return jax.shard_map(
        on_device,
        mesh=mesh,
        in_specs=placed,
        out_specs=(P("seq", "head"), P("seq", "head"), P("seq", "head"), P("seq", "head")),
        check_vma=False,
    )
```

profile of v0, /device:TPU:28, one launch (start us, length us, event | category | flops | bytes accessed | tf_op | source)
XLA Modules:
  0.0 664.9 jit_solution(17443305365971809694)
XLA Ops:
  7.2 1.0 copy.92
  9.1 1.0 copy.64
  10.9 1.1 fusion.3
  12.1 159.0 %all-gather.5.cloned.1.call-done = f32[192,128,128]{2,1,0:T(8,128)} async-done(((f32[2,128,128]{2,1,0:T(8,128)}), f32[192,128,128]{2,1,0:T(8,128)}) %all-gather.5.cloned.1.call-update) | async-done | bytes 12582928 | tf_op jit(solution)/shard_map/all_gather | solution.py:12
  171.1 93.4 %while.28 = (s32[]{:T(128)}, f32[2,128,128]{2,1,0:T(8,128)S(1)}, s32[]{:T(128)}, f32[96,2,128,128]{3,2,1,0:T(8,128)}, s32[]{:T(128)}, /*index=5*/s32[]{:T(128)}) while((s32[]{:T(128)}, f32[2,128,128]{2,1,0:T(8,128)S(1)}, s32[]{:T(128)}, f32[96,2,128,128]{3,2,1,0:T(8,128)}, s32[]{:T(128)}, /*index=5*/s32[]{:T(128)}) %tuple.82), condition=%wide.region_1.2_spmd.clone, body=%wide.region_0.1_spmd.clone.sunk | while | flops 98308 | bytes 393317 | solution.py:20
  172.1 0.9 add_select_fusion.4
  173.1 0.9 add_select_fusion.4
  174.1 0.9 add_select_fusion.4
  175.0 0.9 add_select_fusion.4
  176.0 0.9 add_select_fusion.4
  177.0 0.9 add_select_fusion.4
  177.9 0.9 add_select_fusion.4
  178.9 0.9 add_select_fusion.4
  179.9 0.9 add_select_fusion.4
  180.9 0.9 add_select_fusion.4
  181.8 0.9 add_select_fusion.4
  182.8 0.9 add_select_fusion.4
  183.8 0.9 add_select_fusion.4
  184.8 0.9 add_select_fusion.4
  185.7 0.9 add_select_fusion.4
  186.7 0.9 add_select_fusion.4
  187.7 0.9 add_select_fusion.4
  265.9 10.6 %all-reduce = (f32[128]{0:T(128)S(1)}, f32[128]{0:T(128)S(1)}) all-reduce(f32[128]{0:T(128)S(1)} %get-tuple-element.228, f32[128]{0:T(128)S(1)} %multiply_reduce_fusion), channel_id=1, replica_groups=mesh['seq'=96,'head'=8] {'head'}, use_global_device_ids=true, to_apply=%region_3.4 | all-reduce | flops 256 | bytes 2048 | tf_op jit(solution)/shard_map/psum | solution.py:50
  276.4 1.6 subtract_convert_fusion.1
  280.6 148.0 %all-gather.7.cloned.1.call-done = f32[192,128,128]{2,1,0:T(8,128)} async-done(((f32[2,128,128]{2,1,0:T(8,128)}), f32[192,128,128]{2,1,0:T(8,128)}) %all-gather.7.cloned.1.call-update) | async-done | bytes 12582928 | tf_op jit(solution)/shard_map/all_gather | solution.py:12
  428.6 93.4 %while.29 = (s32[]{:T(128)}, f32[2,128,128]{2,1,0:T(8,128)S(1)}, s32[]{:T(128)}, f32[96,2,128,128]{3,2,1,0:T(8,128)}, s32[]{:T(128)}, /*index=5*/s32[]{:T(128)}) while((s32[]{:T(128)}, f32[2,128,128]{2,1,0:T(8,128)S(1)}, s32[]{:T(128)}, f32[96,2,128,128]{3,2,1,0:T(8,128)}, s32[]{:T(128)}, /*index=5*/s32[]{:T(128)}) %tuple.81), condition=%wide.region_8.9_spmd.clone, body=%wide.region_7.8_spmd.clone.sunk | while | flops 98308 | bytes 393317 | solution.py:20
  444.2 1.0 add_select_fusion.5
  445.2 1.0 add_select_fusion.5
  449.0 1.0 add_select_fusion.5
  450.0 1.0 add_select_fusion.5
  455.9 1.0 add_select_fusion.5
  456.8 1.0 add_select_fusion.5
  458.8 1.0 add_select_fusion.5
  459.8 1.0 add_select_fusion.5
  461.7 1.0 add_select_fusion.5
  462.7 1.0 add_select_fusion.5
  463.7 1.0 add_select_fusion.5
  465.6 1.0 add_select_fusion.5
  466.6 1.0 add_select_fusion.5
  467.5 1.0 add_select_fusion.5
  468.5 1.0 add_select_fusion.5
  469.5 1.0 add_select_fusion.5
  470.5 1.0 add_select_fusion.5
  472.4 1.0 add_select_fusion.5
  473.4 1.0 add_select_fusion.5
  476.3 1.0 add_select_fusion.5
  477.3 1.0 add_select_fusion.5
  478.3 1.0 add_select_fusion.5
  479.2 1.0 add_select_fusion.5
  480.2 1.0 add_select_fusion.5
  483.1 1.0 add_select_fusion.5
  484.1 1.0 add_select_fusion.5
  486.1 1.0 add_select_fusion.5
  487.0 1.0 add_select_fusion.5
  488.0 1.0 add_select_fusion.5
  489.0 1.0 add_select_fusion.5
  508.4 1.0 add_select_fusion.5
  509.4 1.0 add_select_fusion.5
  519.1 1.0 add_select_fusion.5
  520.1 1.0 add_select_fusion.5
  521.1 1.0 add_select_fusion.5
  522.2 132.3 %all-reduce.3.cloned.1.call-done = f32[2,128,128]{1,2,0:T(8,128)} async-done(((f32[2,128,128]{1,2,0:T(8,128)}), f32[2,128,128]{1,2,0:T(8,128)}) %all-reduce.3.cloned.1.call-update) | async-done | bytes 131088 | tf_op jit(solution)/shard_map/psum | solution.py:58
  654.5 1.0 subtract_convert_fusion
  655.7 1.0 fusion.6
  (172 shorter events, 140.7 us)
Async XLA Ops:
  7.2 1.0 copy-start
  7.2 164.0 %all-gather.5.cloned.1.call-start = ((), (), s32[]{:S(2)}) async-start(), calls=%async_computation.1 | async-start | bytes 12713984 | tf_op jit(solution)/shard_map/all_gather | solution.py:12
  9.0 419.6 %all-gather.7.cloned.1.call-start = ((), (), s32[]{:S(2)}) async-start(), calls=%async_computation.2 | async-start | bytes 12713984 | tf_op jit(solution)/shard_map/all_gather | solution.py:12
  278.3 2.3 copy-start.1
  279.1 375.4 %all-reduce.3.cloned.1.call-start = ((), (), s32[]{:S(2)}) async-start(), calls=%async_computation | async-start | bytes 262144 | tf_op jit(solution)/shard_map/psum | solution.py:58
Sparse Core Ops, SparseCore 0:
  11.7 159.3 all-gather.4
  279.2 149.3 all-gather.6
  432.3 222.1 all-reduce.2
where the time goes:
time: 669 us; the launch traced here: 665 us
  waiting for transfers between devices  439 us (66%)
  other arithmetic  187 us (28%)
  between operations  13.9 us (2%)
  blocking collectives  10.6 us (2%)
    all_gather x2, waiting for transfers between devices, carried_in(): everything = lax.all_gather(value, axis)  307 us
    select_n x192, other arithmetic, turn(): return jnp.where(reached, new, before)  182 us
    psum x1, waiting for transfers between devices, on_device(): overall = lax.psum(grad_local, 'seq')  132 us
  transfers between devices with their start and end apart: 3, of which 3 were waited for; matrix products, arithmetic and copies ran while one was open for 14% of the time, Pallas kernels for 0%

commit v1 on v0

--- a/solution.py
+++ b/solution.py
@@ -5,23 +5,64 @@
 
 HD = 128
 D = 2048
+NY, NZ = 8, 12
+BY, BZ = 4, 4
+AY, AZ = NY // BY, NZ // BZ
+MEMBERS = BY * BZ
+BLOCKS = AY * AZ
+ROWS = 2 * HD // MEMBERS
+
+INSIDE = [
+    [(BY * a + i) * NZ + BZ * b + j for i in range(BY) for j in range(BZ)]
+    for a in range(AY)
+    for b in range(AZ)
+]
+ACROSS = [
+    [(BY * a + i) * NZ + BZ * b + j for a in range(AY) for b in range(AZ)]
+    for i in range(BY)
+    for j in range(BZ)
+]
 
 
-def carried_in(value, axis, combine, identity):
-    count, position = (lax.axis_size(axis), lax.axis_index(axis))
-    everything = lax.all_gather(value, axis)
-    start = jnp.broadcast_to(jnp.asarray(identity, value.dtype), value.shape)
-
-    def turn(k, before):
-        reached = k < position
-        new = combine(before, everything[k])
-        return jnp.where(reached, new, before)
-
-    return lax.fori_loop(0, count, turn, start)
-
-
-def add_states(earlier, later_term):
-    return earlier + later_term
+def carried(local, later):
+    position = lax.axis_index("seq")
+    a = (position // NZ) // BY
+    b = (position % NZ) // BZ
+    parts = local.reshape(MEMBERS, ROWS, HD)
+    parts = lax.all_to_all(parts, "seq", 0, 0, axis_index_groups=INSIDE)
+    parts = parts.reshape(BY, BZ, ROWS, HD)
+    row = jnp.sum(parts, axis=1)
+    block = jnp.arange(BLOCKS)
+    to_a, to_b = block // AZ, block % AZ
+    if later:
+        whole = to_a < a
+        same_row = (to_a == a) & (to_b < b)
+    else:
+        whole = to_a > a
+        same_row = (to_a == a) & (to_b > b)
+    same = to_a == a
+    own = jnp.arange(BY)
+    other = own[None, :] > own[:, None] if later else own[None, :] < own[:, None]
+    eye = own[None, :] == own[:, None]
+    counted = (
+        whole[:, None, None]
+        | (same[:, None, None] & other[None])
+        | (same_row[:, None, None] & eye[None])
+    )
+    sent = jnp.sum(jnp.where(counted[:, :, :, None, None], row[None, None], 0.0), axis=2)
+    got = lax.all_to_all(sent, "seq", 0, 0, axis_index_groups=ACROSS)
+    base = jnp.sum(got, axis=0)
+    out = []
+    order = range(BZ - 1, -1, -1) if later else range(BZ)
+    running = base
+    for j in order:
+        running = running + parts[:, j]
+        out.append(running)
+    if later:
+        out = out[::-1]
+    back = jnp.stack(out, axis=1).reshape(MEMBERS, ROWS, HD)
+    back = lax.all_to_all(back, "seq", 0, 0, axis_index_groups=INSIDE)
+    return back.reshape(local.shape) - local
 
 
 def on_device(queries, keys, values, grad_out, gain, segment_ids):
@@ -40,24 +81,21 @@
     raw_scores = jnp.einsum("thd,shd->hts", queries_h, keys_h, preferred_element_type=jnp.float32)
     scores = (raw_scores * allowed[None]).astype(jnp.bfloat16)
     local_state = jnp.einsum("thd,the->hde", keys_h, values_h, preferred_element_type=jnp.float32)
-    zero_state = jnp.zeros_like(local_state)
-    state = carried_in(local_state, "seq", add_states, zero_state)
+    state = carried(local_state, False)
     state_b = state.astype(jnp.bfloat16)
     attn = jnp.einsum("hts,she->the", scores, values_h, preferred_element_type=jnp.float32)
     attn = attn + jnp.einsum("thd,hde->the", queries_h, state_b, preferred_element_type=jnp.float32)
     flat = attn.reshape(length, width)
     gained = gain * grad_out.astype(jnp.float32)
-    squares, products = lax.psum(
-        (jnp.sum(flat * flat, axis=1), jnp.sum(gained * flat, axis=1)), "head"
-    )
+    own = jnp.stack([jnp.sum(flat * flat, axis=1), jnp.sum(gained * flat, axis=1)])
+    own = jnp.broadcast_to(own[None], (8, 2, length))
+    squares, products = jnp.sum(lax.all_to_all(own, "head", 0, 0), axis=0)
     inverse = lax.rsqrt(squares / D + 1e-06)
     output = (gain * flat * inverse[:, None]).astype(jnp.bfloat16)
     dflat = gained * inverse[:, None] - flat * (products * inverse**3 / D)[:, None]
     dattn = dflat.astype(jnp.bfloat16).reshape(length, heads_here, HD)
     grad_local = jnp.einsum("thd,the->hde", queries_h, dattn, preferred_element_type=jnp.float32)
-    overall = lax.psum(grad_local, "seq")
-    before = carried_in(grad_local, "seq", add_states, zero_state)
-    later = overall - before - grad_local
+    later = carried(grad_local, True)
     later_b = later.astype(jnp.bfloat16)
     dscores = (
         jnp.einsum("the,she->hts", dattn, values_h, preferred_element_type=jnp.float32)

time: 669 us -> 124 us (0.19)
  the two profiles are of different devices: /device:TPU:28 before, /device:TPU:8 now
where the time goes in v1:
time: 124 us; the launch traced here: 123 us
  waiting for transfers between devices  50.2 us (40%)
  starting transfers between devices  38.5 us (31%)
  blocking collectives  20.7 us (17%)
  local copies, waits for them, and re-layouts  6.23 us (5%)
  other arithmetic  3.85 us (3%)
  matrix products  2.85 us (2%)
    all_to_all x2, waiting for transfers between devices, carried(): got = lax.all_to_all(sent, 'seq', 0, 0, axis_index_groups=ACROSS)  29.7 us
    all_to_all x2, starting transfers between devices, carried(): got = lax.all_to_all(sent, 'seq', 0, 0, axis_index_groups=ACROSS)  15.9 us
    all_to_all x2, waiting for transfers between devices, carried(): back = lax.all_to_all(back, 'seq', 0, 0, axis_index_groups=INSIDE)  13.3 us
    all_to_all x1, starting transfers between devices, carried(): parts = lax.all_to_all(parts, 'seq', 0, 0, axis_index_groups=INSIDE)  12.8 us
    all_to_all x1, blocking collectives, carried(): parts = lax.all_to_all(parts, 'seq', 0, 0, axis_index_groups=INSIDE)  11.3 us
    all_to_all x2, starting transfers between devices, carried(): back = lax.all_to_all(back, 'seq', 0, 0, axis_index_groups=INSIDE)  9.82 us
    all_to_all x1, blocking collectives, on_device(): squares, products = jnp.sum(lax.all_to_all(own, 'head', 0, 0), axis=0)  9.42 us
    all_to_all x1, waiting for transfers between devices, carried(): parts = lax.all_to_all(parts, 'seq', 0, 0, axis_index_groups=INSIDE)  7.19 us
  transfers between devices with their start and end apart: 5, of which 5 were waited for; matrix products, arithmetic and copies ran while one was open for 2% of the time, Pallas kernels for 0%

profile of v1, /device:TPU:8, one launch (start us, length us, event | category | flops | bytes accessed | tf_op | source)
XLA Modules:
  0.0 123.2 jit_solution(12869055804744474207)
XLA Ops:
  0.6 0.0 copy-start
  0.6 1.0 copy.168
  1.6 0.0 copy-done
  1.6 0.8 fusion.13
  2.4 12.8 %all-to-all-start = ((f32[16,16,128]{2,1,0:T(8,128)}), f32[16,16,128]{2,1,0:T(8,128)S(1)}, u32[]{:S(2)}, u32[]{:S(2)}) async-start(f32[16,16,128]{2,1,0:T(8,128)} %bitcast.2), calls=%async_computation | async-start | bytes 262144 | tf_op jit(solution)/shard_map/all_to_all | solution.py:32
  15.3 0.1 and_or_fusion
  15.4 7.2 %all-to-all-done = f32[16,16,128]{2,1,0:T(8,128)S(1)} async-done(((f32[16,16,128]{2,1,0:T(8,128)}), f32[16,16,128]{2,1,0:T(8,128)S(1)}, u32[]{:S(2)}, u32[]{:S(2)}) %all-to-all-start) | async-done | bytes 131104 | tf_op jit(solution)/shard_map/all_to_all | solution.py:32
  22.6 0.8 select_reduce_fusion.1
  23.4 0.0 copy-start.3
  23.4 11.9 %all-to-all-start.1 = ((f32[6,4,16,128]{3,2,1,0:T(8,128)}), f32[6,4,16,128]{3,2,1,0:T(8,128)S(1)}, u32[]{:S(2)}, u32[]{:S(2)}) async-start(f32[6,4,16,128]{3,2,1,0:T(8,128)} %select_reduce_fusion.1), calls=%async_computation.1 | async-start | bytes 393216 | tf_op jit(solution)/shard_map/all_to_all | solution.py:53
  35.3 0.0 copy-done.3
  35.3 0.1 copy.140
  35.4 0.0 copy-start.5
  35.4 0.7 copy-done.5
  36.1 0.1 fusion.18
  36.2 14.6 %all-to-all-done.1 = f32[6,4,16,128]{3,2,1,0:T(8,128)S(1)} async-done(((f32[6,4,16,128]{3,2,1,0:T(8,128)}), f32[6,4,16,128]{3,2,1,0:T(8,128)S(1)}, u32[]{:S(2)}, u32[]{:S(2)}) %all-to-all-start.1) | async-done | bytes 196640 | tf_op jit(solution)/shard_map/all_to_all | solution.py:53
  50.8 0.6 copy.101
  51.5 0.0 copy-start.1
  51.5 4.9 %all-to-all-start.2 = ((f32[16,16,128]{2,1,0:T(8,128)}), f32[16,16,128]{2,1,0:T(8,128)S(1)}, u32[]{:S(2)}, u32[]{:S(2)}) async-start(f32[16,16,128]{2,1,0:T(8,128)} %bitcast.5), calls=%async_computation.2 | async-start | bytes 262144 | tf_op jit(solution)/shard_map/all_to_all | solution.py:64
  56.3 0.0 copy-done.1
  56.3 0.2 fusion.3
  56.6 0.2 convolution_bitcast_fusion.5
  56.8 7.0 %all-to-all-done.2 = f32[16,16,128]{2,1,0:T(8,128)S(1)} async-done(((f32[16,16,128]{2,1,0:T(8,128)}), f32[16,16,128]{2,1,0:T(8,128)S(1)}, u32[]{:S(2)}, u32[]{:S(2)}) %all-to-all-start.2) | async-done | bytes 131104 | tf_op jit(solution)/shard_map/all_to_all | solution.py:64
  63.7 0.9 fusion.9
  64.7 0.2 multiply_reduce_fusion.1
  64.9 0.0 copy-start.2
  64.9 0.0 copy-start.4
  64.9 0.1 copy.104
  65.0 0.7 copy-done.2
  65.7 0.0 copy-done.4
  65.8 0.1 multiply_reduce_fusion
  65.9 9.4 %all_to_all.35 = f32[8,2,128]{2,1,0:T(2,128)S(1)} all-to-all(f32[8,2,128]{2,1,0:T(2,128)S(1)} %broadcast_in_dim.46), channel_id=1, replica_groups=mesh['seq'=96,'head'=8] {'head'}, dimensions={0} | all-to-all | bytes 16384 | tf_op jit(solution)/shard_map/all_to_all | solution.py:92
  75.3 0.7 subtract_convert_fusion
  76.1 0.1 copy.141
  76.2 0.2 fusion.42
  76.4 11.3 %all_to_all.36 = f32[16,16,128]{2,1,0:T(8,128)S(1)} all-to-all(f32[16,16,128]{2,1,0:T(8,128)S(1)} %bitcast.169), channel_id=1, replica_groups={{0,8,16,24,96,104,112,120,192,200,208,216,288,296,304,312},{32,40,48,56..., dimensions={0} | all-to-all | bytes 262144 | tf_op jit(solution)/shard_map/all_to_all | solution.py:32
  87.7 0.8 select_reduce_fusion
  88.5 4.0 %all-to-all-start.5 = ((f32[6,4,16,128]{3,2,1,0:T(8,128)}), f32[6,4,16,128]{3,2,1,0:T(8,128)S(1)}, u32[]{:S(2)}, u32[]{:S(2)}) async-start(f32[6,4,16,128]{3,2,1,0:T(8,128)} %select_reduce_fusion), calls=%async_computation.5 | async-start | bytes 393216 | tf_op jit(solution)/shard_map/all_to_all | solution.py:53
  92.6 0.2 fusion.4
  92.8 0.2 convolution_bitcast_fusion.3
  93.0 15.1 %all-to-all-done.5 = f32[6,4,16,128]{3,2,1,0:T(8,128)S(1)} async-done(((f32[6,4,16,128]{3,2,1,0:T(8,128)}), f32[6,4,16,128]{3,2,1,0:T(8,128)S(1)}, u32[]{:S(2)}, u32[]{:S(2)}) %all-to-all-start.5) | async-done | bytes 196640 | tf_op jit(solution)/shard_map/all_to_all | solution.py:53
  108.2 0.6 copy.119
  108.8 5.0 %all-to-all-start.6 = ((f32[16,16,128]{2,1,0:T(8,128)}), f32[16,16,128]{2,1,0:T(8,128)S(1)}, u32[]{:S(2)}, u32[]{:S(2)}) async-start(f32[16,16,128]{2,1,0:T(8,128)} %bitcast.21), calls=%async_computation.6 | async-start | bytes 262144 | tf_op jit(solution)/shard_map/all_to_all | solution.py:64
  113.8 0.2 fusion.5
  113.9 0.7 copy.124
  114.7 0.1 fusion.41
  114.8 6.4 %all-to-all-done.6 = f32[16,16,128]{2,1,0:T(8,128)S(1)} async-done(((f32[16,16,128]{2,1,0:T(8,128)}), f32[16,16,128]{2,1,0:T(8,128)S(1)}, u32[]{:S(2)}, u32[]{:S(2)}) %all-to-all-start.6) | async-done | bytes 131104 | tf_op jit(solution)/shard_map/all_to_all | solution.py:64
  121.2 0.2 convolution_bitcast_fusion.1
  121.3 0.2 fusion.6
  121.6 0.7 copy.126
  122.3 0.2 fusion.7
  122.5 0.7 copy.125
  (19 shorter events, 0.2 us)
Async XLA Ops:
  0.6 1.0 copy-start
  2.4 20.2 %all-to-all-start = ((f32[16,16,128]{2,1,0:T(8,128)}), f32[16,16,128]{2,1,0:T(8,128)S(1)}, u32[]{:S(2)}, u32[]{:S(2)}) async-start(f32[16,16,128]{2,1,0:T(8,128)} %bitcast.2), calls=%async_computation | async-start | bytes 262144 | tf_op jit(solution)/shard_map/all_to_all | solution.py:32
  23.4 11.9 %copy-start.3 = (bf16[128,256]{1,0:T(8,128)(2,1)S(1)}, bf16[128,256]{1,0:T(8,128)(2,1)}, u32[]{:S(2)}) copy-start(bf16[128,256]{1,0:T(8,128)(2,1)} %param.6) | copy-start | bytes 196612
  23.4 27.3 %all-to-all-start.1 = ((f32[6,4,16,128]{3,2,1,0:T(8,128)}), f32[6,4,16,128]{3,2,1,0:T(8,128)S(1)}, u32[]{:S(2)}, u32[]{:S(2)}) async-start(f32[6,4,16,128]{3,2,1,0:T(8,128)} %select_reduce_fusion.1), calls=%async_computation.1 | async-start | bytes 393216 | tf_op jit(solution)/shard_map/all_to_all | solution.py:53
  35.4 0.7 copy-start.5
  51.5 4.9 %copy-start.1 = (bf16[128,256]{1,0:T(8,128)(2,1)S(1)}, bf16[128,256]{1,0:T(8,128)(2,1)}, u32[]{:S(2)}) copy-start(bf16[128,256]{1,0:T(8,128)(2,1)} %param.7) | copy-start | bytes 196612
  51.5 12.3 %all-to-all-start.2 = ((f32[16,16,128]{2,1,0:T(8,128)}), f32[16,16,128]{2,1,0:T(8,128)S(1)}, u32[]{:S(2)}, u32[]{:S(2)}) async-start(f32[16,16,128]{2,1,0:T(8,128)} %bitcast.5), calls=%async_computation.2 | async-start | bytes 262144 | tf_op jit(solution)/shard_map/all_to_all | solution.py:64
  64.9 0.8 copy-start.2
  64.9 0.8 copy-start.4
  88.5 19.6 %all-to-all-start.5 = ((f32[6,4,16,128]{3,2,1,0:T(8,128)}), f32[6,4,16,128]{3,2,1,0:T(8,128)S(1)}, u32[]{:S(2)}, u32[]{:S(2)}) async-start(f32[6,4,16,128]{3,2,1,0:T(8,128)} %select_reduce_fusion), calls=%async_computation.5 | async-start | bytes 393216 | tf_op jit(solution)/shard_map/all_to_all | solution.py:53
  108.8 12.4 %all-to-all-start.6 = ((f32[16,16,128]{2,1,0:T(8,128)}), f32[16,16,128]{2,1,0:T(8,128)S(1)}, u32[]{:S(2)}, u32[]{:S(2)}) async-start(f32[16,16,128]{2,1,0:T(8,128)} %bitcast.21), calls=%async_computation.6 | async-start | bytes 262144 | tf_op jit(solution)/shard_map/all_to_all | solution.py:64

commit v2 on v0

--- a/solution.py
+++ b/solution.py
@@ -1,27 +1,84 @@
+import functools
+
 import jax
 import jax.numpy as jnp
 from jax import lax
+from jax.experimental import pallas as pl
+from jax.experimental.pallas import tpu as pltpu
 from jax.sharding import PartitionSpec as P
 
 HD = 128
 D = 2048
+NY, NZ = 8, 12
+BZ = 4
+AZ = NZ // BZ
+MEMBERS = NY * BZ
+ROWS = 2 * HD // MEMBERS
+
+ORDER = [26, 17, 11, 10, 28, 1, 5, 4, 7, 16, 9, 19, 30, 13, 22, 0, 21, 29, 6, 12, 20, 23, 14, 15, 3, 31, 2, 24, 25, 27, 18, 8]
+SLOT = [[ORDER.index(BZ * y + z) for z in range(BZ)] for y in range(NY)]
+INSIDE = [[(k // BZ) * NZ + BZ * b + k % BZ for k in ORDER] for b in range(AZ)]
+ACROSS = [
+    [y * NZ + BZ * b + z for b in range(AZ)][:: 1 if z % 2 else -1]
+    for y in range(NY)
+    for z in range(BZ)
+]
 
 
-def carried_in(value, axis, combine, identity):
-    count, position = (lax.axis_size(axis), lax.axis_index(axis))
-    everything = lax.all_gather(value, axis)
-    start = jnp.broadcast_to(jnp.asarray(identity, value.dtype), value.shape)
-
-    def turn(k, before):
-        reached = k < position
-        new = combine(before, everything[k])
-        return jnp.where(reached, new, before)
-
-    return lax.fori_loop(0, count, turn, start)
+def spread_kernel(later, parts_ref, sent_ref):
+    column = lax.axis_index("seq") % NZ
+    b = column // BZ
+    flip = 1 - column % 2
+    rows = []
+    for y in range(NY):
+        row = parts_ref[SLOT[y][0]]
+        for z in range(1, BZ):
+            row = row + parts_ref[SLOT[y][z]]
+        rows.append(row)
+    running = jnp.zeros_like(rows[0])
+    for y in range(NY - 1, -1, -1) if later else range(NY):
+        for to in range(AZ):
+            dest = jnp.where(flip == 1, AZ - 1 - to, to)
+            takes = dest < b if later else dest > b
+            sent_ref[to, y] = running + jnp.where(takes, rows[y], 0.0)
+        running = running + rows[y]
 
 
-def add_states(earlier, later_term):
-    return earlier + later_term
+def finish_kernel(later, parts_ref, got_ref, back_ref):
+    for y in range(NY):
+        running = got_ref[0, y]
+        for src in range(1, AZ):
+            running = running + got_ref[src, y]
+        for z in range(BZ - 1, -1, -1) if later else range(BZ):
+            running = running + parts_ref[SLOT[y][z]]
+            back_ref[SLOT[y][z]] = running
+
+
+def in_vmem(x):
+    return pltpu.with_memory_space_constraint(x, pltpu.VMEM)
+
+
+def carried(local, later):
+    vmem = pl.BlockSpec(memory_space=pltpu.VMEM)
+    parts = local.reshape(MEMBERS, ROWS, HD)
+    parts = lax.all_to_all(parts, "seq", 0, 0, axis_index_groups=INSIDE)
+    sent = pl.pallas_call(
+        functools.partial(spread_kernel, later),
+        out_shape=pltpu.VMEM((AZ, NY, ROWS, HD), jnp.float32),
+        in_specs=[vmem],
+        out_specs=vmem,
+        name="spread_later" if later else "spread",
+    )(in_vmem(parts))
+    got = lax.all_to_all(sent, "seq", 0, 0, axis_index_groups=ACROSS)
+    back = pl.pallas_call(
+        functools.partial(finish_kernel, later),
+        out_shape=pltpu.VMEM((MEMBERS, ROWS, HD), jnp.float32),
+        in_specs=[vmem, vmem],
+        out_specs=vmem,
+        name="finish_later" if later else "finish",
+    )(in_vmem(parts), in_vmem(got))
+    back = lax.all_to_all(back, "seq", 0, 0, axis_index_groups=INSIDE)
+    return back.reshape(local.shape) - local
 
 
 def on_device(queries, keys, values, grad_out, gain, segment_ids):
@@ -40,24 +97,21 @@
     raw_scores = jnp.einsum("thd,shd->hts", queries_h, keys_h, preferred_element_type=jnp.float32)
     scores = (raw_scores * allowed[None]).astype(jnp.bfloat16)
     local_state = jnp.einsum("thd,the->hde", keys_h, values_h, preferred_element_type=jnp.float32)
-    zero_state = jnp.zeros_like(local_state)
-    state = carried_in(local_state, "seq", add_states, zero_state)
+    state = carried(local_state, False)
     state_b = state.astype(jnp.bfloat16)
     attn = jnp.einsum("hts,she->the", scores, values_h, preferred_element_type=jnp.float32)
     attn = attn + jnp.einsum("thd,hde->the", queries_h, state_b, preferred_element_type=jnp.float32)
     flat = attn.reshape(length, width)
     gained = gain * grad_out.astype(jnp.float32)
-    squares, products = lax.psum(
-        (jnp.sum(flat * flat, axis=1), jnp.sum(gained * flat, axis=1)), "head"
-    )
+    own = jnp.stack([jnp.sum(flat * flat, axis=1), jnp.sum(gained * flat, axis=1)])
+    own = jnp.broadcast_to(own[None], (8, 2, length))
+    squares, products = jnp.sum(lax.all_to_all(own, "head", 0, 0), axis=0)
     inverse = lax.rsqrt(squares / D + 1e-06)
     output = (gain * flat * inverse[:, None]).astype(jnp.bfloat16)
     dflat = gained * inverse[:, None] - flat * (products * inverse**3 / D)[:, None]
     dattn = dflat.astype(jnp.bfloat16).reshape(length, heads_here, HD)
     grad_local = jnp.einsum("thd,the->hde", queries_h, dattn, preferred_element_type=jnp.float32)
-    overall = lax.psum(grad_local, "seq")
-    before = carried_in(grad_local, "seq", add_states, zero_state)
-    later = overall - before - grad_local
+    later = carried(grad_local, True)
     later_b = later.astype(jnp.bfloat16)
     dscores = (
         jnp.einsum("the,she->hts", dattn, values_h, preferred_element_type=jnp.float32)

time: 669 us -> 113 us (0.17)
  the two profiles are of different devices: /device:TPU:28 before, /device:TPU:8 now
where the time goes in v2:
time: 113 us
  starting transfers between devices  60.1 us (53%)
  waiting for transfers between devices  28.3 us (25%)
  blocking collectives  9.41 us (8%)
  local copies, waits for them, and re-layouts  4.94 us (4%)
  matrix products  3.5 us (3%)
  other arithmetic  2.81 us (2%)
  Pallas kernels  2.67 us (2%)
    all_to_all x2, starting transfers between devices, carried(): parts = lax.all_to_all(parts, 'seq', 0, 0, axis_index_groups=INSIDE)  24.7 us
    all_to_all x2, starting transfers between devices, carried(): back = lax.all_to_all(back, 'seq', 0, 0, axis_index_groups=INSIDE)  18.1 us
    all_to_all x2, starting transfers between devices, carried(): got = lax.all_to_all(sent, 'seq', 0, 0, axis_index_groups=ACROSS)  17.4 us
    all_to_all x2, waiting for transfers between devices, carried(): parts = lax.all_to_all(parts, 'seq', 0, 0, axis_index_groups=INSIDE)  9.81 us
    all_to_all x2, waiting for transfers between devices, carried(): got = lax.all_to_all(sent, 'seq', 0, 0, axis_index_groups=ACROSS)  9.81 us
    all_to_all x1, blocking collectives, on_device(): squares, products = jnp.sum(lax.all_to_all(own, 'head', 0, 0), axis=0)  9.41 us
    all_to_all x2, waiting for transfers between devices, carried(): back = lax.all_to_all(back, 'seq', 0, 0, axis_index_groups=INSIDE)  8.67 us
    unnamed x15, local copies, waits for them, and re-layouts  3.64 us
  transfers between devices with their start and end apart: 6, of which 6 were waited for; matrix products, arithmetic and copies ran while one was open for 2% of the time, Pallas kernels for 0%

profile of v2, /device:TPU:8, one launch (start us, length us, event | category | flops | bytes accessed | tf_op | source)
XLA Modules:
  0.0 112.6 jit_solution(12951030830831262735)
XLA Ops:
  0.6 0.0 copy-start
  0.6 1.0 copy.116
  1.6 0.0 copy-done
  1.6 0.8 fusion.13
  2.4 0.0 copy-start.3
  2.4 16.4 %all-to-all-start = ((f32[32,8,128]{2,1,0:T(8,128)}), f32[32,8,128]{2,1,0:T(8,128)S(1)}, u32[]{:S(2)}, u32[]{:S(2)}) async-start(f32[32,8,128]{2,1,0:T(8,128)} %bitcast.2), calls=%async_computation | async-start | bytes 262144 | tf_op jit(solution)/shard_map/all_to_all | solution.py:64
  18.8 0.0 copy-done.3
  18.8 0.1 copy.88
  18.9 5.0 %all-to-all-done.parts_ref = f32[32,8,128]{2,1,0:T(8,128)S(1)} async-done(((f32[32,8,128]{2,1,0:T(8,128)}), f32[32,8,128]{2,1,0:T(8,128)S(1)}, u32[]{:S(2)}, u32[]{:S(2)}) %all-to-all-start) | async-done | bytes 131104 | tf_op jit(solution)/shard_map/all_to_all | solution.py:64
  23.9 0.7 spread.1
  24.6 10.2 %all-to-all-start.1 = ((f32[3,8,8,128]{3,2,1,0:T(8,128)}), f32[3,8,8,128]{3,2,1,0:T(8,128)S(1)}, u32[]{:S(2)}, u32[]{:S(2)}) async-start(f32[3,8,8,128]{3,2,1,0:T(8,128)} %spread.1), calls=%async_computation.1 | async-start | bytes 196608 | tf_op jit(solution)/shard_map/all_to_all | solution.py:72
  34.7 0.0 copy-start.5
  34.7 0.7 copy-done.5
  35.4 0.1 fusion.18
  35.5 4.5 %all-to-all-done.1.got_ref = f32[3,8,8,128]{3,2,1,0:T(8,128)S(1)} async-done(((f32[3,8,8,128]{3,2,1,0:T(8,128)}), f32[3,8,8,128]{3,2,1,0:T(8,128)S(1)}, u32[]{:S(2)}, u32[]{:S(2)}) %all-to-all-start.1) | async-done | bytes 98336 | tf_op jit(solution)/shard_map/all_to_all | solution.py:72
  40.0 0.7 finish.1
  40.7 0.0 copy-start.1
  40.7 9.5 %all-to-all-start.2 = ((f32[32,8,128]{2,1,0:T(8,128)}), f32[32,8,128]{2,1,0:T(8,128)S(1)}, u32[]{:S(2)}, u32[]{:S(2)}) async-start(f32[32,8,128]{2,1,0:T(8,128)} %finish.1), calls=%async_computation.2 | async-start | bytes 262144 | tf_op jit(solution)/shard_map/all_to_all | solution.py:80
  50.2 0.0 copy-done.1
  50.2 0.2 fusion.3
  50.4 0.2 convolution_bitcast_fusion.5
  50.6 4.6 %all-to-all-done.2 = f32[32,8,128]{2,1,0:T(8,128)S(1)} async-done(((f32[32,8,128]{2,1,0:T(8,128)}), f32[32,8,128]{2,1,0:T(8,128)S(1)}, u32[]{:S(2)}, u32[]{:S(2)}) %all-to-all-start.2) | async-done | bytes 131104 | tf_op jit(solution)/shard_map/all_to_all | solution.py:80
  55.3 0.9 fusion.9
  56.2 0.2 multiply_reduce_fusion.1
  56.4 0.0 copy-start.2
  56.5 0.0 copy-start.4
  56.5 0.1 copy.65
  56.6 0.7 copy-done.2
  57.3 0.0 copy-done.4
  57.3 0.1 multiply_reduce_fusion
  57.4 9.4 %all_to_all.35 = f32[8,2,128]{2,1,0:T(2,128)S(1)} all-to-all(f32[8,2,128]{2,1,0:T(2,128)S(1)} %broadcast_in_dim.12), channel_id=1, replica_groups=mesh['seq'=96,'head'=8] {'head'}, dimensions={0} | all-to-all | bytes 16384 | tf_op jit(solution)/shard_map/all_to_all | solution.py:108
  66.9 0.7 subtract_convert_fusion
  67.6 0.1 copy.89
  67.7 0.8 fusion.28
  68.6 8.3 %all-to-all-start.4 = ((f32[32,8,128]{2,1,0:T(8,128)}), f32[32,8,128]{2,1,0:T(8,128)S(1)}, u32[]{:S(2)}, u32[]{:S(2)}) async-start(f32[32,8,128]{2,1,0:T(8,128)} %bitcast.15), calls=%async_computation.4 | async-start | bytes 262144 | tf_op jit(solution)/shard_map/all_to_all | solution.py:64
  76.9 0.2 fusion.4
  77.1 4.9 %all-to-all-done.4.parts_ref = f32[32,8,128]{2,1,0:T(8,128)S(1)} async-done(((f32[32,8,128]{2,1,0:T(8,128)}), f32[32,8,128]{2,1,0:T(8,128)S(1)}, u32[]{:S(2)}, u32[]{:S(2)}) %all-to-all-start.4) | async-done | bytes 131104 | tf_op jit(solution)/shard_map/all_to_all | solution.py:64
  82.0 0.7 spread_later.1
  82.6 7.2 %all-to-all-start.5 = ((f32[3,8,8,128]{3,2,1,0:T(8,128)}), f32[3,8,8,128]{3,2,1,0:T(8,128)S(1)}, u32[]{:S(2)}, u32[]{:S(2)}) async-start(f32[3,8,8,128]{3,2,1,0:T(8,128)} %spread_later.1), calls=%async_computation.5 | async-start | bytes 196608 | tf_op jit(solution)/shard_map/all_to_all | solution.py:72
  89.8 0.2 convolution_bitcast_fusion.3
  90.0 5.3 %all-to-all-done.5.got_ref = f32[3,8,8,128]{3,2,1,0:T(8,128)S(1)} async-done(((f32[3,8,8,128]{3,2,1,0:T(8,128)}), f32[3,8,8,128]{3,2,1,0:T(8,128)S(1)}, u32[]{:S(2)}, u32[]{:S(2)}) %all-to-all-start.5) | async-done | bytes 98336 | tf_op jit(solution)/shard_map/all_to_all | solution.py:72
  95.3 0.7 finish_later.1
  95.9 8.6 %all-to-all-start.6 = ((f32[32,8,128]{2,1,0:T(8,128)}), f32[32,8,128]{2,1,0:T(8,128)S(1)}, u32[]{:S(2)}, u32[]{:S(2)}) async-start(f32[32,8,128]{2,1,0:T(8,128)} %finish_later.1), calls=%async_computation.6 | async-start | bytes 262144 | tf_op jit(solution)/shard_map/all_to_all | solution.py:80
  104.5 0.2 fusion.5
  104.7 0.7 copy.80
  105.4 0.1 fusion.27
  105.6 4.0 %all-to-all-done.6 = f32[32,8,128]{2,1,0:T(8,128)S(1)} async-done(((f32[32,8,128]{2,1,0:T(8,128)}), f32[32,8,128]{2,1,0:T(8,128)S(1)}, u32[]{:S(2)}, u32[]{:S(2)}) %all-to-all-start.6) | async-done | bytes 131104 | tf_op jit(solution)/shard_map/all_to_all | solution.py:80
  109.6 0.9 fusion.8
  110.5 0.2 convolution_bitcast_fusion.1
  110.7 0.2 fusion.6
  110.9 0.7 copy.82
  111.7 0.2 fusion.7
  111.8 0.7 copy.81
  (5 shorter events, 0.0 us)
Async XLA Ops:
  0.6 1.0 copy-start
  2.4 16.4 %copy-start.3 = (bf16[128,256]{1,0:T(8,128)(2,1)S(1)}, bf16[128,256]{1,0:T(8,128)(2,1)}, u32[]{:S(2)}) copy-start(bf16[128,256]{1,0:T(8,128)(2,1)} %param.6) | copy-start | bytes 196612
  2.4 21.5 %all-to-all-start = ((f32[32,8,128]{2,1,0:T(8,128)}), f32[32,8,128]{2,1,0:T(8,128)S(1)}, u32[]{:S(2)}, u32[]{:S(2)}) async-start(f32[32,8,128]{2,1,0:T(8,128)} %bitcast.2), calls=%async_computation | async-start | bytes 262144 | tf_op jit(solution)/shard_map/all_to_all | solution.py:64
  24.6 15.4 %all-to-all-start.1 = ((f32[3,8,8,128]{3,2,1,0:T(8,128)}), f32[3,8,8,128]{3,2,1,0:T(8,128)S(1)}, u32[]{:S(2)}, u32[]{:S(2)}) async-start(f32[3,8,8,128]{3,2,1,0:T(8,128)} %spread.1), calls=%async_computation.1 | async-start | bytes 196608 | tf_op jit(solution)/shard_map/all_to_all | solution.py:72
  34.7 0.7 copy-start.5
  40.7 9.5 %copy-start.1 = (bf16[128,256]{1,0:T(8,128)(2,1)S(1)}, bf16[128,256]{1,0:T(8,128)(2,1)}, u32[]{:S(2)}) copy-start(bf16[128,256]{1,0:T(8,128)(2,1)} %param.7) | copy-start | bytes 196612
  40.7 14.6 %all-to-all-start.2 = ((f32[32,8,128]{2,1,0:T(8,128)}), f32[32,8,128]{2,1,0:T(8,128)S(1)}, u32[]{:S(2)}, u32[]{:S(2)}) async-start(f32[32,8,128]{2,1,0:T(8,128)} %finish.1), calls=%async_computation.2 | async-start | bytes 262144 | tf_op jit(solution)/shard_map/all_to_all | solution.py:80
  56.4 0.8 copy-start.2
  56.5 0.8 copy-start.4
  68.6 13.4 %all-to-all-start.4 = ((f32[32,8,128]{2,1,0:T(8,128)}), f32[32,8,128]{2,1,0:T(8,128)S(1)}, u32[]{:S(2)}, u32[]{:S(2)}) async-start(f32[32,8,128]{2,1,0:T(8,128)} %bitcast.15), calls=%async_computation.4 | async-start | bytes 262144 | tf_op jit(solution)/shard_map/all_to_all | solution.py:64
  82.6 12.6 %all-to-all-start.5 = ((f32[3,8,8,128]{3,2,1,0:T(8,128)}), f32[3,8,8,128]{3,2,1,0:T(8,128)S(1)}, u32[]{:S(2)}, u32[]{:S(2)}) async-start(f32[3,8,8,128]{3,2,1,0:T(8,128)} %spread_later.1), calls=%async_computation.5 | async-start | bytes 196608 | tf_op jit(solution)/shard_map/all_to_all | solution.py:72
  95.9 13.7 %all-to-all-start.6 = ((f32[32,8,128]{2,1,0:T(8,128)}), f32[32,8,128]{2,1,0:T(8,128)S(1)}, u32[]{:S(2)}, u32[]{:S(2)}) async-start(f32[32,8,128]{2,1,0:T(8,128)} %finish_later.1), calls=%async_computation.6 | async-start | bytes 262144 | tf_op jit(solution)/shard_map/all_to_all | solution.py:80
